TPU v7x, 128 devices: a whole 4x4x4 slice. The times are simulated.
128 devices in a mesh: ctx: 16 (over y_hi, x, core), vocab: 8 (over y_lo, z).
Axes of the slice: x: 4, y: 4 (y_hi: 2, y_lo: 2; y = y_hi * 2 + y_lo), z: 4, core: 2. Of those that a mesh axis runs over, the one named last changes fastest.
Arguments:
- block_query: bfloat16 [512, 6144], P('ctx', 'vocab'), may hold values from -16 to 16
- block_key: bfloat16 [512, 6144], P('ctx', 'vocab'), may hold values from -16 to 16
- block_value: bfloat16 [512, 6144], P('ctx', 'vocab'), may hold values from -6 to 6
- block_doc: int32 [512], P('ctx'), may hold values from 0 to 1, never falling along the last dimension, each value on 1 to 480 neighbouring positions
- token_query: bfloat16 [2048, 6144], P(('ctx', 'vocab')), may hold values from -16 to 16
- token_key: bfloat16 [2048, 6144], P(('ctx', 'vocab')), may hold values from -16 to 16
- token_value: bfloat16 [2048, 6144], P(('ctx', 'vocab')), may hold values from -600 to 600
- token_state: bfloat16 [2048, 6144], P(('ctx', 'vocab')), may hold values from -6 to 6
- norm_gain: float32 [6144], replicated, may hold values from 0.5 to 1.5
- head_weight: bfloat16 [6144, 131072], P(None, ('ctx', 'vocab')), may hold values from -128 to 128
- targets: int32 [2048], replicated, may hold values from 0 to 131071
Outputs:
- block_context: bfloat16 [512, 6144], P('ctx', 'vocab')
- token_prior: float32 [2048], P(('ctx', 'vocab'))
Inputs may be any that keep to these rules, and one draw needn't show every extreme that they name: block_doc never falls along the blocks; no document holds more than 480 blocks.
All inputs are finite; a program needn't handle non-finite values.
Results may differ from a plain program's by a relative error of at most 0.005.
Values may be sent and summed in bfloat16 or wider, within the bound.
No kernel may reach another device: no remote copies, remote signals or barrier semaphores. Data moves between devices by JAX's collectives and lax.ppermute only.
A program may use at most 128 MiB of HBM per device.

v0:
```python
import math

import jax
import jax.numpy as jnp
from jax import lax
from jax.sharding import Mesh
from jax.sharding import PartitionSpec as P

HEAD_DIM = 128
BLOCK_LEN = 4
CTX = ("ctx_0", "ctx_1", "ctx_2")
VOCAB = ("vocab_0", "vocab_1")
CTX_VOCAB = ("ctx_0", "ctx_1", "ctx_2", "vocab_0", "vocab_1")


big_negative = -1e30


def sent_to_all(value, axis):
    size = lax.axis_size(axis)
    return lax.all_to_all(
        jnp.broadcast_to(value[None], (size, *value.shape)), axis, 0, 0, tiled=True
    )


def joined_along(pieces, dim):
    pieces = jnp.moveaxis(pieces, 0, dim)
    shape = pieces.shape
    return pieces.reshape(*shape[:dim], shape[dim] * shape[dim + 1], *shape[dim + 2 :])


def gathered_copies(value, axis, dim):
    pieces = sent_to_all(value, axis)
    return joined_along(pieces, dim)


def all_in_one(value, axis):
    leaves = jax.tree.leaves(value)
    sequence = sorted(range(len(leaves)), key=lambda k: -leaves[k].size)
    width = (1, *leaves[sequence[0]].shape)[-1]
    lines = [
        jnp.pad(leaves[k].reshape(-1), (0, -leaves[k].size % width)).reshape(-1, width)
        for k in sequence
    ]
    both, at, found = (lax.all_gather(jnp.concatenate(lines), axis), 0, {})
    for k, line in zip(sequence, lines):
        share = both[:, at : at + len(line)].reshape(len(both), -1)
        found[k] = share[:, : leaves[k].size].reshape(-1, *leaves[k].shape)
        at += len(line)
    numbers = iter(range(len(leaves)))
    return jax.tree.map(lambda _: found[next(numbers)], value)


def merged_by_axis(value, axes, combine):
    for axis in axes:
        pieces = all_in_one(value, axis)
        value = jax.tree.map(lambda part: part[0], pieces)
        for k in range(1, lax.axis_size(axis)):
            value = combine(value, jax.tree.map(lambda part: part[k], pieces))
    return value


def local_decoder(context, token_query, token_key, token_value, token_state, norm_gain):
    scale = 1.0 / math.sqrt(HEAD_DIM)
    groups = context.shape[0]
    width = context.shape[1]
    head_total = width // HEAD_DIM
    shape = (groups, BLOCK_LEN, head_total, HEAD_DIM)
    prefix = context.reshape(groups, 1, head_total, HEAD_DIM)
    queries = token_query.reshape(shape)
    keys = jnp.concatenate([prefix, token_key.reshape(shape)], axis=1)
    values = jnp.concatenate([prefix, token_value.reshape(shape)], axis=1)
    scores = (
        jnp.einsum("bihd,bjhd->bhij", queries, keys, preferred_element_type=jnp.float32) * scale
    )
    allowed = (
        jnp.arange(BLOCK_LEN + 1, dtype=jnp.int32)[None, :]
        <= jnp.arange(BLOCK_LEN, dtype=jnp.int32)[:, None] + 1
    )
    scores = jnp.where(allowed, scores, -jnp.inf)
    highest = jnp.max(scores, axis=-1, keepdims=True)
    weights = jnp.exp(scores - highest)
    totals = jnp.sum(weights, axis=-1)
    mixed = jnp.einsum(
        "bhij,bjhd->bihd", weights.astype(jnp.bfloat16), values, preferred_element_type=jnp.float32
    )
    mixed = mixed / jnp.transpose(totals, (0, 2, 1))[..., None]
    summed = token_state.astype(jnp.float32) + mixed.reshape(groups * BLOCK_LEN, width)
    power = jnp.mean(summed * summed, axis=-1, keepdims=True)
    return (summed * lax.rsqrt(power + 1e-05) * norm_gain).astype(jnp.bfloat16)


def local(
    block_query,
    block_key,
    block_value,
    block_doc,
    token_query,
    token_key,
    token_value,
    token_state,
    norm_gain,
    head_weight,
    targets,
):
    local_rows = block_query.shape[0]
    head_count = block_query.shape[1] // HEAD_DIM
    scale = 1.0 / math.sqrt(HEAD_DIM)
    first_row = lax.axis_index(CTX) * local_rows
    queries = block_query.reshape(local_rows, head_count, HEAD_DIM)
    own_doc = block_doc.astype(jnp.bfloat16)
    query_places = first_row + jnp.arange(local_rows, dtype=jnp.int32)
    highest = jnp.full((local_rows, head_count), big_negative, jnp.float32)
    keys = lax.all_gather(block_key, CTX, axis=0, tiled=True)
    values = lax.all_gather(block_value, CTX, axis=0, tiled=True)
    docs = lax.all_gather(own_doc, CTX, axis=0, tiled=True)
    count = keys.shape[0]
    keys = keys.reshape(count, head_count, HEAD_DIM)
    values = values.reshape(count, head_count, HEAD_DIM)
    scores = jnp.einsum("qhd,khd->qhk", queries, keys, preferred_element_type=jnp.float32) * scale
    key_places = jnp.arange(count, dtype=jnp.int32)
    allowed = (query_places[:, None] >= key_places[None, :]) & (own_doc[:, None] == docs[None, :])
    allowed = allowed[:, None, :]
    newest = jnp.maximum(highest, jnp.max(jnp.where(allowed, scores, big_negative), axis=-1))
    weights = jnp.where(allowed, jnp.exp(scores - newest[..., None]), 0.0)
    totals = jnp.sum(weights, axis=-1)
    update = jnp.einsum(
        "qhk,khd->qhd", weights.astype(jnp.bfloat16), values, preferred_element_type=jnp.float32
    )
    mixed = update
    highest, totals, mixed = (newest, totals, mixed)
    block_context = (
        (mixed / totals[..., None]).reshape(local_rows, head_count * HEAD_DIM).astype(jnp.bfloat16)
    )
    grouped = lax.all_to_all(block_context, VOCAB, split_axis=0, concat_axis=1, tiled=True)
    hidden = local_decoder(grouped, token_query, token_key, token_value, token_state, norm_gain)
    vocab_cols = head_weight.shape[1]
    col_start = lax.axis_index(CTX_VOCAB) * vocab_cols
    columns = jnp.arange(vocab_cols, dtype=jnp.int32)
    group_states = gathered_copies(hidden, VOCAB, 0)
    piece = lax.all_gather(group_states, CTX, axis=0, tiled=True)
    logits = jnp.dot(piece, head_weight, preferred_element_type=jnp.float32)
    top = jnp.max(logits, axis=-1)
    mass = jnp.sum(jnp.exp(logits - top[:, None]), axis=-1)
    wanted = targets - col_start
    picked = jnp.sum(jnp.where(columns[None, :] == wanted[:, None], logits, 0.0), axis=1)
    peaks = top
    masses = mass
    picks = picked
    stats = (peaks, masses, picks)

    def combine(left, right):
        top = jnp.maximum(left[0], right[0])
        mass = left[1] * jnp.exp(left[0] - top) + right[1] * jnp.exp(right[0] - top)
        return (top, mass, left[2] + right[2])

    peaks, masses, picks = merged_by_axis(stats, CTX_VOCAB, combine)
    priors = picks - (peaks + jnp.log(masses))
    own_count = hidden.shape[0]
    token_prior = lax.dynamic_slice_in_dim(priors, lax.axis_index(CTX_VOCAB) * own_count, own_count)
    return (block_context, token_prior)


def solution(mesh):
    torus = Mesh(
        mesh.devices.reshape(2, 4, 2, 2, 4), ("ctx_0", "ctx_1", "ctx_2", "vocab_0", "vocab_1")
    )
    in_specs = (
        P(CTX, VOCAB),
        P(CTX, VOCAB),
        P(CTX, VOCAB),
        P(CTX),
        P(CTX_VOCAB, None),
        P(CTX_VOCAB, None),
        P(CTX_VOCAB, None),
        P(CTX_VOCAB, None),
        P(),
        P(None, CTX_VOCAB),
        P(),
    )
    out_specs = (P(CTX, VOCAB), P(CTX_VOCAB))
    return jax.shard_map(local, mesh=torus, in_specs=in_specs, out_specs=out_specs, check_vma=False)
```

profile of v0, /device:TPU:0, one launch (start us, length us, event | category | flops | bytes accessed | tf_op | source)
XLA Modules:
  0.0 360.8 jit_solution(2283637337288649313)
XLA Ops:
  7.2 0.0 copy-start
  7.2 0.0 copy-start.2
  7.2 0.0 copy-start.3
  7.2 0.8 convert_element_type.25
  8.0 1.2 dynamic-slice
  9.9 0.2 dynamic-update-slice
  10.1 38.1 %all-reduce = bf16[512]{0:T(512)(128)(2,1)S(1)} all-reduce(bf16[512]{0:T(512)(128)(2,1)S(1)} %dynamic-update-slice), channel_id=1, replica_groups=mesh['ctx_0'=2,'ctx_1'=4,'ctx_2'=2,'vocab_0'=2,'vocab_1'=4] {'ctx_0','ct..., use_global_device_ids=true, to_apply=%add | all-reduce | flops 512 | bytes 2048
  48.2 21.7 %all_gather.43 = bf16[512,768]{1,0:T(8,128)(2,1)S(1)} all-gather(bf16[32,768]{1,0:T(8,128)(2,1)} %param.12), channel_id=1, replica_groups=mesh['ctx_0'=2,'ctx_1'=4,'ctx_2'=2,'vocab_0'=2,'vocab_1'=4] {'ctx_0','ct..., dimensions={0}, use_global_device_ids=true | all-gather | bytes 835584 | tf_op jit(solution)/shard_map/all_gather | solution.py:114
  69.9 0.3 copy.29
  70.2 0.0 copy-start.4
  70.2 0.1 fusion.19
  70.3 0.0 copy-done
  70.3 0.3 select_reduce_fusion.1
  70.6 23.0 %all_gather.44 = bf16[512,768]{1,0:T(8,128)(2,1)S(1)} all-gather(bf16[32,768]{1,0:T(8,128)(2,1)} %param.13), channel_id=1, replica_groups=mesh['ctx_0'=2,'ctx_1'=4,'ctx_2'=2,'vocab_0'=2,'vocab_1'=4] {'ctx_0','ct..., dimensions={0}, use_global_device_ids=true | all-gather | bytes 835584 | tf_op jit(solution)/shard_map/all_gather | solution.py:115
  93.6 0.3 copy.32
  93.9 0.2 fusion.8
  94.1 0.4 fusion.5
  94.6 0.7 convert_element_type.30
  95.2 5.4 %all-to-all-start = ((bf16[8,4,768]{2,1,0:T(4,128)(2,1)}), bf16[8,4,768]{2,1,0:T(4,128)(2,1)S(1)}, u32[]{:S(2)}, u32[]{:S(2)}) async-start(bf16[8,4,768]{2,1,0:T(4,128)(2,1)} %convert_element_type.30), calls=%async_computation | async-start | bytes 98304 | tf_op jit(solution)/shard_map/all_to_all | solution.py:135
  100.6 0.0 all-gather.12.cloned.1.call-start
  100.7 0.1 iota_compare_fusion.2
  100.8 1.0 copy.48
  101.7 0.1 copy.40
  101.8 0.0 copy-done.2
  101.9 0.0 copy-start.5
  101.9 0.1 copy.38
  102.0 4.9 %all-to-all-done = bf16[8,4,768]{2,1,0:T(4,128)(2,1)S(1)} async-done(((bf16[8,4,768]{2,1,0:T(4,128)(2,1)}), bf16[8,4,768]{2,1,0:T(4,128)(2,1)S(1)}, u32[]{:S(2)}, u32[]{:S(2)}) %all-to-all-start) | async-done | bytes 49184 | tf_op jit(solution)/shard_map/all_to_all | solution.py:135
  107.0 0.5 fusion.61
  107.5 0.5 fusion.10
  108.0 0.6 fusion
  108.6 0.2 multiply_reduce_fusion
  108.9 0.0 copy-done.4
  108.9 0.2 multiply_convert_fusion
  109.0 0.1 broadcast_in_dim.61
  109.2 23.8 %all_to_all.18 = bf16[8,16,6144]{2,1,0:T(8,128)(2,1)} all-to-all(bf16[8,16,6144]{2,1,0:T(8,128)(2,1)S(1)} %broadcast_in_dim.61), channel_id=1, replica_groups=mesh['ctx_0'=2,'ctx_1'=4,'ctx_2'=2,'vocab_0'=2,'vocab_1'=4] {'vocab_0','..., dimensions={0} | all-to-all | bytes 3145728 | tf_op jit(solution)/shard_map/all_to_all | solution.py:21
  133.0 0.0 all-gather.12.cloned.1.call-update
  133.1 0.6 copy_bitcast_fusion
  133.7 143.4 %all-gather.12.cloned.1.call-done = bf16[2048,6144]{1,0:T(8,128)(2,1)} async-done(((bf16[128,6144]{1,0:T(8,128)(2,1)}), bf16[2048,6144]{1,0:T(8,128)(2,1)}) %all-gather.12.cloned.1.call-update) | async-done | bytes 25165840 | tf_op jit(solution)/shard_map/all_gather | solution.py:141
  277.1 34.1 %fusion.62 = (f32[2048]{0:T(1024)S(1)}, f32[2048,1024]{0,1:T(8,128)}) fusion(bf16[2048,6144]{1,0:T(8,128)(2,1)} %all-gather.12.cloned.1.call-done, bf16[6144,1024]{1,0:T(8,128)(2,1)} %param.20), kind=kOutput, calls=%fused_computation.121 | convolution fusion | flops 25771898880 | bytes 46145536 | tf_op jit(solution)/shard_map/dot_general | solution.py:142
  311.2 4.6 %exponential_reduce_fusion = (f32[2048]{0:T(1024)S(1)}, f32[2048]{0:T(1024)S(1)}) fusion(f32[2048,1024]{0,1:T(8,128)} %get-tuple-element.31, f32[2048]{0:T(1024)S(1)} %get-tuple-element.30, s32[2048]{0:T(1024)S(1)} %broadcast_subtract_fusion), kind=kLoop, calls=%fused_computation.2 | loop fusion | flops 10481664 | bytes 8421376 | tf_op jit(solution)/shard_map/reduce_sum | solution.py:144
  315.8 6.1 %all-gather.5 = f32[2,3,2048]{2,1,0:T(4,128)S(1)} all-gather(f32[1,3,2048]{2,1,0:T(4,128)S(1)} %maximum_bitcast_fusion), channel_id=2, replica_groups=mesh['ctx_0'=2,'ctx_1'=4,'ctx_2'=2,'vocab_0'=2,'vocab_1'=4] {'ctx_0'}, dimensions={0}, use_global_device_ids=true | all-gather | bytes 73728 | tf_op jit(solution)/shard_map/all_gather | solution.py:45
  322.0 12.0 %all-gather.6 = f32[4,3,2048]{2,1,0:T(4,128)S(1)} all-gather(f32[1,3,2048]{2,1,0:T(4,128)S(1)} %maximum_bitcast_fusion.1), channel_id=3, replica_groups=mesh['ctx_0'=2,'ctx_1'=4,'ctx_2'=2,'vocab_0'=2,'vocab_1'=4] {'ctx_1'}, dimensions={0}, use_global_device_ids=true | all-gather | bytes 122880 | tf_op jit(solution)/shard_map/all_gather | solution.py:45
  334.0 0.1 fusion.32
  334.2 1.9 all-gather.7
  336.1 4.6 %all-gather.8 = f32[2,3,2048]{2,1,0:T(4,128)S(1)} all-gather(f32[1,3,2048]{2,1,0:T(4,128)S(1)} %maximum_bitcast_fusion.3), channel_id=5, replica_groups=mesh['ctx_0'=2,'ctx_1'=4,'ctx_2'=2,'vocab_0'=2,'vocab_1'=4] {'vocab_0'}, dimensions={0}, use_global_device_ids=true | all-gather | bytes 73728 | tf_op jit(solution)/shard_map/all_gather | solution.py:45
  340.8 12.5 %all-gather.9 = f32[4,3,2048]{2,1,0:T(4,128)S(1)} all-gather(f32[1,3,2048]{2,1,0:T(4,128)S(1)} %maximum_bitcast_fusion.4), channel_id=6, replica_groups=mesh['ctx_0'=2,'ctx_1'=4,'ctx_2'=2,'vocab_0'=2,'vocab_1'=4] {'vocab_1'}, dimensions={0}, use_global_device_ids=true | all-gather | bytes 122880 | tf_op jit(solution)/shard_map/all_gather | solution.py:45
  353.3 0.1 fusion.60
  353.4 0.6 dynamic-slice_subtract_fusion
  (31 shorter events, 0.5 us)
Async XLA Ops:
  7.2 63.1 %copy-start = (bf16[32,768]{1,0:T(8,128)(2,1)S(1)}, bf16[32,768]{1,0:T(8,128)(2,1)}, u32[]{:S(2)}) copy-start(bf16[32,768]{1,0:T(8,128)(2,1)} %param.11) | copy-start | bytes 147460
  7.2 94.6 %copy-start.2 = (bf16[16,6144]{1,0:T(8,128)(2,1)S(1)}, bf16[16,6144]{1,0:T(8,128)(2,1)}, u32[]{:S(2)}) copy-start(bf16[16,6144]{1,0:T(8,128)(2,1)} %param.15) | copy-start | bytes 589828
  7.2 94.7 %copy-start.3 = (bf16[16,6144]{1,0:T(8,128)(2,1)S(1)}, bf16[16,6144]{1,0:T(8,128)(2,1)}, u32[]{:S(2)}) copy-start(bf16[16,6144]{1,0:T(8,128)(2,1)} %param.17) | copy-start | bytes 589828
  69.9 38.7 %copy-start.1 = (bf16[16,6144]{1,0:T(8,128)(2,1)S(1)}, bf16[16,6144]{1,0:T(8,128)(2,1)}, u32[]{:S(2)}) copy-start(bf16[16,6144]{1,0:T(8,128)(2,1)} %param.18) | copy-start | bytes 589828
  70.2 38.7 %copy-start.4 = (f32[6144]{0:T(1024)S(1)}, f32[6144]{0:T(1024)}, u32[]{:S(2)}) copy-start(f32[6144]{0:T(1024)} %param.19) | copy-start | bytes 73732
  95.2 11.7 %all-to-all-start = ((bf16[8,4,768]{2,1,0:T(4,128)(2,1)}), bf16[8,4,768]{2,1,0:T(4,128)(2,1)S(1)}, u32[]{:S(2)}, u32[]{:S(2)}) async-start(bf16[8,4,768]{2,1,0:T(4,128)(2,1)} %convert_element_type.30), calls=%async_computation | async-start | bytes 98304 | tf_op jit(solution)/shard_map/all_to_all | solution.py:135
  100.6 176.4 %all-gather.12.cloned.1.call-start = ((), (), s32[]{:S(2)}) async-start(), calls=%async_computation.2 | async-start | bytes 26738688 | tf_op jit(solution)/shard_map/all_gather | solution.py:141
  101.9 31.2 %copy-start.5 = (s32[2048]{0:T(1024)S(1)}, s32[2048]{0:T(1024)}, u32[]{:S(2)}) copy-start(s32[2048]{0:T(1024)} %param.21) | copy-start | bytes 24580
Sparse Core Ops, SparseCore 0:
  133.2 143.8 all-gather.11
where the time goes:
time: 361 us
  waiting for transfers between devices  148 us (41%)
  blocking collectives  144 us (40%)
  matrix products  35.9 us (10%)
  between operations  15.1 us (4%)
  other arithmetic  7.79 us (2%)
  starting transfers between devices  5.47 us (2%)
  local copies, waits for them, and re-layouts  4.76 us (1%)
    all_gather x1, waiting for transfers between devices, local(): piece = lax.all_gather(group_states, CTX, axis=0, tiled=True)  143 us
    unnamed x1, blocking collectives  38.1 us
    all_gather x5, blocking collectives, all_in_one(): both, at, found = (lax.all_gather(jnp.concatenate(lines), axis), 0, {})  37 us
    dot_general x1, matrix products, local(): logits = jnp.dot(piece, head_weight, preferred_element_type=jnp.float32)  34.1 us
    all_to_all x1, blocking collectives, sent_to_all(): lax.all_to_all(jnp.broadcast_to(value[None], (size, *value.shape)), axis,...  23.8 us
    all_gather x1, blocking collectives, local(): values = lax.all_gather(block_value, CTX, axis=0, tiled=True)  23 us
    all_gather x1, blocking collectives, local(): keys = lax.all_gather(block_key, CTX, axis=0, tiled=True)  21.7 us
  transfers between devices with their start and end apart: 2, of which 2 were waited for; matrix products, arithmetic and copies ran while one was open for 1% of the time, Pallas kernels for 0%

commit v1 on v0

v1 whole, which is shorter than its diff:
```python
import functools
import math

import jax
import jax.numpy as jnp
from jax import lax
from jax.experimental import pallas as pl
from jax.experimental.pallas import tpu as pltpu
from jax.sharding import Mesh
from jax.sharding import PartitionSpec as P


HEAD_DIM = 128
BLOCK_LEN = 4
CTX = ("ctx_0", "ctx_1", "ctx_2")
VOCAB = ("vocab_0", "vocab_1")
CTX_VOCAB = ("ctx_0", "ctx_1", "ctx_2", "vocab_0", "vocab_1")

big_negative = -1e30
LANES = 128
K_STEP = 1536


def moved(value, step):
    pairs = []
    for yh in range(2):
        for x in range(4):
            for c in range(2):
                for yl in range(2):
                    for z in range(4):
                        x2, y2, z2, c2 = step(x, yh * 2 + yl, z, c)
                        x2, y2, z2 = x2 % 4, y2 % 4, z2 % 4
                        src = (((yh * 4 + x) * 2 + c) * 2 + yl) * 4 + z
                        dst = ((((y2 // 2) * 4 + x2) * 2 + c2) * 2 + y2 % 2) * 4 + z2
                        pairs.append((src, dst))
    return lax.ppermute(value, CTX_VOCAB, pairs)


def swapped(value):
    return moved(value, lambda x, y, z, c: (x, y, z, 1 - c))


def along_z(value, d):
    return moved(value, lambda x, y, z, c: (x, y, z + d, c))


def second(value, d):
    return moved(value, lambda x, y, z, c: (x + d * c, y + d * (1 - c), z, c))


def third(value, d):
    return moved(value, lambda x, y, z, c: (x + d * (1 - c), y + d * c, z, c))


def ring_pieces(value, send):
    half = value.shape[0] // 2
    lower = send(value, 1)
    upper = send(value, -1)
    first = send(lower[:half], 1)
    last = send(upper[half:], -1)
    return lower, upper, first, last


def score_kernel(rows, *refs):
    wanted_ref = refs[0]
    pieces = refs[1 : 1 + len(rows)]
    w_ref, out_ref, acc_ref, all_ref = refs[1 + len(rows) :]
    step = pl.program_id(0)
    at = 0
    for piece, count in zip(pieces, rows):
        all_ref[at : at + count, :] = piece[...]
        at += count
    part = jnp.dot(all_ref[...], w_ref[...], preferred_element_type=jnp.float32)

    @pl.when(step == 0)
    def _():
        acc_ref[...] = part

    @pl.when(step > 0)
    def _():
        acc_ref[...] += part

    @pl.when(step == pl.num_programs(0) - 1)
    def _():
        span = 128
        for at in range(0, acc_ref.shape[0], span):
            logits = acc_ref[at : at + span, :]
            top = jnp.max(logits, axis=-1, keepdims=True)
            mass = jnp.sum(jnp.exp(logits - top), axis=-1, keepdims=True)
            column = lax.broadcasted_iota(jnp.int32, logits.shape, 1)
            here = column == wanted_ref[at : at + span, :]
            picked = jnp.sum(jnp.where(here, logits, 0.0), axis=-1, keepdims=True)
            lane = lax.broadcasted_iota(jnp.int32, (span, LANES), 1)
            out_ref[at : at + span, :] = jnp.where(
                lane == 0, top, jnp.where(lane == 1, mass, picked)
            )


def scored(wanted, pieces, head_weight):
    rows = tuple(piece.shape[0] for piece in pieces)
    total = sum(rows)
    depth, columns = head_weight.shape
    return pl.pallas_call(
        functools.partial(score_kernel, rows),
        out_shape=jax.ShapeDtypeStruct((total, LANES), jnp.float32),
        grid=(depth // K_STEP,),
        in_specs=[pl.BlockSpec((total, 1), lambda k: (0, 0))]
        + [pl.BlockSpec((r, K_STEP), lambda k: (0, k)) for r in rows]
        + [pl.BlockSpec((K_STEP, columns), lambda k: (k, 0))],
        out_specs=pl.BlockSpec((total, LANES), lambda k: (0, 0)),
        scratch_shapes=[
            pltpu.VMEM((total, columns), jnp.float32),
            pltpu.VMEM((total, K_STEP), jnp.bfloat16),
        ],
        cost_estimate=pl.CostEstimate(
            flops=2 * total * depth * columns,
            transcendentals=total * columns,
            bytes_accessed=2 * depth * (total + columns),
        ),
        name="scored",
    )(wanted, *pieces, head_weight)


def local_decoder(context, token_query, token_key, token_value, token_state, norm_gain):
    scale = 1.0 / math.sqrt(HEAD_DIM)
    groups = context.shape[0]
    width = context.shape[1]
    head_total = width // HEAD_DIM
    shape = (groups, BLOCK_LEN, head_total, HEAD_DIM)
    prefix = context.reshape(groups, 1, head_total, HEAD_DIM)
    queries = token_query.reshape(shape)
    keys = jnp.concatenate([prefix, token_key.reshape(shape)], axis=1)
    values = jnp.concatenate([prefix, token_value.reshape(shape)], axis=1)
    scores = (
        jnp.einsum("bihd,bjhd->bhij", queries, keys, preferred_element_type=jnp.float32) * scale
    )
    allowed = (
        jnp.arange(BLOCK_LEN + 1, dtype=jnp.int32)[None, :]
        <= jnp.arange(BLOCK_LEN, dtype=jnp.int32)[:, None] + 1
    )
    scores = jnp.where(allowed, scores, -jnp.inf)
    highest = jnp.max(scores, axis=-1, keepdims=True)
    weights = jnp.exp(scores - highest)
    totals = jnp.sum(weights, axis=-1)
    mixed = jnp.einsum(
        "bhij,bjhd->bihd", weights.astype(jnp.bfloat16), values, preferred_element_type=jnp.float32
    )
    mixed = mixed / jnp.transpose(totals, (0, 2, 1))[..., None]
    summed = token_state.astype(jnp.float32) + mixed.reshape(groups * BLOCK_LEN, width)
    power = jnp.mean(summed * summed, axis=-1, keepdims=True)
    return (summed * lax.rsqrt(power + 1e-05) * norm_gain).astype(jnp.bfloat16)


def gathered_blocks(block_key, block_value, block_doc):
    rows, width = block_key.shape
    row = jnp.arange(rows, dtype=jnp.int32)
    lane = jnp.arange(LANES, dtype=jnp.int32)[None, :]
    place = lax.axis_index(CTX)
    facts = jnp.where(
        lane == 0, block_doc[:, None], jnp.where(lane == 1, place, row[:, None])
    ).astype(jnp.bfloat16)
    own = jnp.concatenate([block_key, block_value, facts], axis=1)
    across = moved(own, lambda x, y, z, c: (x, y + 2, z, c))
    mine = jnp.concatenate([own, across])
    chip = jnp.concatenate([mine, swapped(mine)])

    def by_core(x, y, z, c):
        return (x + 1 - 2 * c, y, z, c)

    near = moved(chip, by_core)
    far = moved(near[: mine.shape[0]], by_core)
    found = jnp.concatenate([chip, near, swapped(near), far, swapped(far)])
    facts = found[:, 2 * width :].astype(jnp.int32)
    docs = facts[:, 0]
    places = facts[:, 1] * rows + facts[:, 2]
    return found[:, :width], found[:, width : 2 * width], docs, places


def local(
    block_query,
    block_key,
    block_value,
    block_doc,
    token_query,
    token_key,
    token_value,
    token_state,
    norm_gain,
    head_weight,
    targets,
):
    local_rows = block_query.shape[0]
    head_count = block_query.shape[1] // HEAD_DIM
    scale = 1.0 / math.sqrt(HEAD_DIM)
    queries = block_query.reshape(local_rows, head_count, HEAD_DIM)
    query_places = lax.axis_index(CTX) * local_rows + jnp.arange(local_rows, dtype=jnp.int32)
    keys, values, docs, key_places = gathered_blocks(block_key, block_value, block_doc)
    count = keys.shape[0]
    keys = keys.reshape(count, head_count, HEAD_DIM)
    values = values.reshape(count, head_count, HEAD_DIM)
    scores = jnp.einsum("qhd,khd->qhk", queries, keys, preferred_element_type=jnp.float32) * scale
    allowed = (query_places[:, None] >= key_places[None, :]) & (
        block_doc[:, None] == docs[None, :]
    )
    allowed = allowed[:, None, :]
    newest = jnp.max(jnp.where(allowed, scores, big_negative), axis=-1)
    weights = jnp.where(allowed, jnp.exp(scores - newest[..., None]), 0.0)
    totals = jnp.sum(weights, axis=-1)
    mixed = jnp.einsum(
        "qhk,khd->qhd", weights.astype(jnp.bfloat16), values, preferred_element_type=jnp.float32
    )
    block_context = (
        (mixed / totals[..., None]).reshape(local_rows, head_count * HEAD_DIM).astype(jnp.bfloat16)
    )
    grouped = lax.all_to_all(block_context, VOCAB, split_axis=0, concat_axis=1, tiled=True)
    hidden = local_decoder(grouped, token_query, token_key, token_value, token_state, norm_gain)

    own_count = hidden.shape[0]
    yh, x, c, yl, z = (lax.axis_index(name) for name in CTX_VOCAB)
    y = yh * 2 + yl
    offset = jnp.array([0, -1, 1, 2], jnp.int32)
    call_third = jnp.array([[0] * 4, [-1, -1, 1, 1], [-1, -1, 1, 1], [2] * 4], jnp.int32)
    call_second = jnp.array(
        [[0, -1, 1, 2], [0, -1, 1, 2], [1, 2, 0, -1], [0, -1, 1, 2]], jnp.int32
    )
    d3, core, d2, d1 = (
        call_third[:, None, :, None],
        jnp.stack([c, 1 - c])[None, :, None, None],
        call_second[:, None, :, None],
        offset[None, None, None, :],
    )
    x_of = (x + jnp.where(core == 0, d3, d2)) % 4
    y_of = (y + jnp.where(core == 0, d2, d3)) % 4
    z_of = (z + d1) % 4
    ids = ((((y_of // 2) * 4 + x_of) * 2 + core) * 2 + y_of % 2) * 4 + z_of
    devices = ids.size
    ids = ids.reshape(devices)
    spread = (ids[:, None] == jnp.arange(devices, dtype=jnp.int32)[None, :]).astype(jnp.float32)
    wanted = jnp.dot(
        spread, targets.reshape(devices, own_count).astype(jnp.float32), precision="highest"
    ).astype(jnp.int32)
    vocab_cols = head_weight.shape[1]
    wanted = wanted - lax.axis_index(CTX_VOCAB) * vocab_cols
    wanted = wanted.reshape(4, -1, 1)

    line = [hidden, along_z(hidden, 1), along_z(hidden, -1), along_z(hidden, 2)]
    line = jnp.concatenate(line)
    plane = jnp.concatenate([line, *ring_pieces(line, second)])
    half = plane.shape[0] // 2

    lower_0 = third(plane[:half], 1)
    upper_1 = third(plane[half:], -1)
    lower_1 = third(plane[half:], 1)
    upper_0 = third(plane[:half], -1)
    first = third(lower_0, 1)
    last = third(upper_1, -1)
    results = []
    for k, pieces in enumerate(([plane], [lower_0, upper_1], [lower_1, upper_0], [first, last])):
        others = [swapped(piece) for piece in pieces]
        results.append(scored(wanted[k], [*pieces, *others], head_weight))
    stats = jnp.concatenate(results)[:, :3]
    stats = stats.reshape(devices, own_count, 3).transpose(0, 2, 1).reshape(devices, 3 * own_count)
    stats = jnp.dot(spread.T, stats, precision="highest")
    stats = lax.all_to_all(stats, CTX_VOCAB, split_axis=0, concat_axis=0, tiled=True)
    stats = stats.reshape(devices, 3, own_count)
    tops = stats[:, 0]
    top = jnp.max(tops, axis=0)
    mass = jnp.sum(stats[:, 1] * jnp.exp(tops - top), axis=0)
    token_prior = jnp.sum(stats[:, 2], axis=0) - (top + jnp.log(mass))
    return (block_context, token_prior)


def solution(mesh):
    torus = Mesh(
        mesh.devices.reshape(2, 4, 2, 2, 4), ("ctx_0", "ctx_1", "ctx_2", "vocab_0", "vocab_1")
    )
    in_specs = (
        P(CTX, VOCAB),
        P(CTX, VOCAB),
        P(CTX, VOCAB),
        P(CTX),
        P(CTX_VOCAB, None),
        P(CTX_VOCAB, None),
        P(CTX_VOCAB, None),
        P(CTX_VOCAB, None),
        P(),
        P(None, CTX_VOCAB),
        P(),
    )
    out_specs = (P(CTX, VOCAB), P(CTX_VOCAB))
    return jax.shard_map(local, mesh=torus, in_specs=in_specs, out_specs=out_specs, check_vma=False)
```

time: 361 us -> 224 us (0.62)
  blocking collectives: 144 us -> 0 us
  Pallas kernels: 0 us -> 51.3 us
  waiting for transfers between devices: 148 us -> 101 us
  starting transfers between devices: 5.47 us -> 40.8 us
  matrix products: 35.9 us -> 2.89 us
  local copies, waits for them, and re-layouts: 4.76 us -> 20 us
  between operations: 15.1 us -> 1.12 us
    all_gather x1 -> x0, waiting for transfers between devices: 143 us -> none  [local(): piece = lax.all_gather(group_states, CTX, axis=0, tiled=True)]
    ppermute x0 -> x26, waiting for transfers between devices: none -> 86.1 us  [moved(): return lax.ppermute(value, CTX_VOCAB, pairs)]
    all_gather x7 -> x0, blocking collectives: 81.6 us -> none  [the longest x5 37 us: all_in_one(): both, at, found = (lax.all_gather(jnp.concatenate(lines), axis), 0, {})]
    pallas_call x0 -> x4, Pallas kernels: none -> 51.3 us  [scored(): pl.pallas_call(functools.partial(score_kernel, rows), out_shape=jax.Shape...]
    unnamed x1 -> x0, blocking collectives: 38.1 us -> none
    dot_general x1 -> x2, matrix products: 34.1 us -> 1.18 us  [the longest x1 0.95 us: local(): stats = jnp.dot(spread.T, stats, precision='highest')]
    ppermute x0 -> x26, starting transfers between devices: none -> 27.2 us  [moved(): return lax.ppermute(value, CTX_VOCAB, pairs)]
    all_to_all x1 -> x0, blocking collectives: 23.8 us -> none  [sent_to_all(): lax.all_to_all(jnp.broadcast_to(value[None], (size, *value.shape)), axis,...]
  transfers between devices with their start and end apart: 2 -> 28, of which waited for: 2 -> 13; matrix products, arithmetic and copies ran while one was open for 1% -> 5% of each run, Pallas kernels for 0% -> 17%
where the time goes in v1:
time: 224 us; the launch traced here: 223 us
  waiting for transfers between devices  101 us (45%)
  Pallas kernels  51.3 us (23%)
  starting transfers between devices  40.8 us (18%)
  local copies, waits for them, and re-layouts  20 us (9%)
  other arithmetic  6.41 us (3%)
  matrix products  2.89 us (1%)
    ppermute x26, waiting for transfers between devices, moved(): return lax.ppermute(value, CTX_VOCAB, pairs)  86.1 us
    pallas_call x4, Pallas kernels, scored(): pl.pallas_call(functools.partial(score_kernel, rows), out_shape=jax.Shape...  51.3 us
    ppermute x26, starting transfers between devices, moved(): return lax.ppermute(value, CTX_VOCAB, pairs)  27.2 us
    all_to_all x1, waiting for transfers between devices, local(): lax.all_to_all(stats, CTX_VOCAB, split_axis=0, concat_axis=0, tiled=True)  8.88 us
    unnamed x46, local copies, waits for them, and re-layouts  7.65 us
    all_to_all x1, starting transfers between devices, local(): lax.all_to_all(stats, CTX_VOCAB, split_axis=0, concat_axis=0, tiled=True)  7.28 us
    all_to_all x1, starting transfers between devices, local(): lax.all_to_all(block_context, VOCAB, split_axis=0, concat_axis=1, tiled=T...  6.38 us
    all_to_all x1, waiting for transfers between devices, local(): lax.all_to_all(block_context, VOCAB, split_axis=0, concat_axis=1, tiled=T...  5.93 us
  transfers between devices with their start and end apart: 28, of which 13 were waited for; matrix products, arithmetic and copies ran while one was open for 5% of the time, Pallas kernels for 17%

profile of v1, /device:TPU:0, one launch (start us, length us, event | category | flops | bytes accessed | tf_op | source)
XLA Modules:
  0.0 223.5 jit_solution(3674517449264277708)
XLA Ops:
  0.7 0.7 select_convert_fusion
  1.4 0.8 pad_maximum_fusion.10
  2.5 3.4 %collective-permute-start = (bf16[32,1664]{0,1:T(8,128)(2,1)S(1)}, bf16[32,1664]{0,1:T(8,128)(2,1)S(1)}, u32[]{:S(2)}, u32[]{:S(2)}) collective-permute-start(bf16[32,1664]{0,1:T(8,128)(2,1)S(1)} %copy.76), channel_id=1, source_target_pairs={{0,64},{1,65},{2,66},{3,67},{4,68},{5,69},{6,70},{7,71},{8,72},{9,... | collective-permute-start | bytes 319496 | tf_op jit(solution)/shard_map/ppermute | solution.py:36
  5.9 9.8 %collective-permute-done = bf16[32,1664]{0,1:T(8,128)(2,1)S(1)} collective-permute-done((bf16[32,1664]{0,1:T(8,128)(2,1)S(1)}, bf16[32,1664]{0,1:T(8,128)(2,1)S(1)}, u32[]{:S(2)}, u32[]{:S(2)}) %collective-permute-start) | collective-permute-done | bytes 106528 | tf_op jit(solution)/shard_map/ppermute | solution.py:36
  16.0 1.8 collective-permute-done.1
  18.2 1.6 collective-permute-start.2
  19.8 7.8 %collective-permute-done.2 = bf16[128,1664]{0,1:T(8,128)(2,1)S(1)} collective-permute-done((bf16[128,1664]{0,1:T(8,128)(2,1)S(1)}, bf16[128,1664]{0,1:T(8,128)(2,1)S(1)}, u32[]{:S(2)}, u32[]{:S(2)}) %collective-permute-start.2) | collective-permute-done | bytes 426016 | tf_op jit(solution)/shard_map/ppermute | solution.py:36
  27.9 1.2 collective-permute-start.3
  29.1 7.8 %collective-permute-done.4 = bf16[64,1664]{0,1:T(8,128)(2,1)S(1)} collective-permute-done((bf16[64,1664]{0,1:T(8,128)(2,1)S(1)}, bf16[64,1664]{0,1:T(8,128)(2,1)S(1)}, u32[]{:S(2)}, u32[]{:S(2)}) %collective-permute-start.4) | collective-permute-done | bytes 213024 | tf_op jit(solution)/shard_map/ppermute | solution.py:36
  37.0 1.7 collective-permute-done.5
  38.7 0.8 copy-done.3
  39.5 5.0 %concatenate.43 = bf16[512,1664]{0,1:T(8,128)(2,1)S(1)} concatenate(bf16[32,1664]{0,1:T(8,128)(2,1)S(1)} %copy.76, bf16[32,1664]{0,1:T(8,128)(2,1)S(1)} %collective-permute-done, bf16[64,1664]{0,1:T(8,128)(2,1)S(1)} %collective-permute-done.1, bf16[128,1664]{0,1:T(8,128)(2,1)S(1)} %collective-permute-done.2, bf16[128,1664]{0,1:T(8,128)(2,1)} %collective-permute-done.3, ...), dimensions={0} | concatenate | bytes 3407872 | tf_op jit(solution)/shard_map/concatenate | solution.py:172
  46.6 6.4 %all-to-all-start = ((bf16[8,4,768]{2,1,0:T(4,128)(2,1)}), bf16[8,4,768]{2,1,0:T(4,128)(2,1)S(1)}, u32[]{:S(2)}, u32[]{:S(2)}) async-start(bf16[8,4,768]{2,1,0:T(4,128)(2,1)} %convert_element_type.47), calls=%async_computation | async-start | bytes 98304 | tf_op jit(solution)/shard_map/all_to_all | solution.py:215
  53.4 5.9 %all-to-all-done = bf16[8,4,768]{2,1,0:T(4,128)(2,1)S(1)} async-done(((bf16[8,4,768]{2,1,0:T(4,128)(2,1)}), bf16[8,4,768]{2,1,0:T(4,128)(2,1)S(1)}, u32[]{:S(2)}, u32[]{:S(2)}) %all-to-all-start) | async-done | bytes 49184 | tf_op jit(solution)/shard_map/all_to_all | solution.py:215
  61.5 0.8 constant_dynamic-update-slice_fusion.7
  62.9 2.7 %collective-permute-start.7 = (bf16[16,6144]{1,0:T(8,128)(2,1)S(1)}, bf16[16,6144]{1,0:T(8,128)(2,1)S(1)}, u32[]{:S(2)}, u32[]{:S(2)}) collective-permute-start(bf16[16,6144]{1,0:T(8,128)(2,1)S(1)} %get-tuple-element.5), channel_id=1, source_target_pairs={{0,3},{1,0},{2,1},{3,2},{4,7},{5,4},{6,5},{7,6},{8,11},{9,8},{10,9... | collective-permute-start | bytes 589832 | tf_op jit(solution)/shard_map/ppermute | solution.py:36
  65.6 7.8 %collective-permute-done.6 = bf16[16,6144]{1,0:T(8,128)(2,1)S(1)} collective-permute-done((bf16[16,6144]{1,0:T(8,128)(2,1)S(1)}, bf16[16,6144]{1,0:T(8,128)(2,1)S(1)}, u32[]{:S(2)}, u32[]{:S(2)}) %collective-permute-start.6) | collective-permute-done | bytes 196640 | tf_op jit(solution)/shard_map/ppermute | solution.py:36
  73.5 0.7 collective-permute-start.9
  74.2 2.6 %collective-permute-start.10 = (bf16[64,6144]{1,0:T(8,128)(2,1)S(1)}, bf16[64,6144]{1,0:T(8,128)(2,1)S(1)}, u32[]{:S(2)}, u32[]{:S(2)}) collective-permute-start(bf16[64,6144]{1,0:T(8,128)(2,1)S(1)} %pad_maximum_fusion.3), channel_id=1, source_target_pairs={{0,68},{1,69},{2,70},{3,71},{4,0},{5,1},{6,2},{7,3},{8,56},{9,57},... | collective-permute-start | bytes 2359304 | tf_op jit(solution)/shard_map/ppermute | solution.py:36
  76.8 0.7 constant_dynamic-update-slice_fusion.6
  77.5 0.7 constant_dynamic-update-slice_fusion.5
  78.2 0.7 constant_dynamic-update-slice_fusion.4
  78.9 7.8 %collective-permute-done.9 = bf16[64,6144]{1,0:T(8,128)(2,1)S(1)} collective-permute-done((bf16[64,6144]{1,0:T(8,128)(2,1)S(1)}, bf16[64,6144]{1,0:T(8,128)(2,1)S(1)}, u32[]{:S(2)}, u32[]{:S(2)}) %collective-permute-start.9) | collective-permute-done | bytes 786464 | tf_op jit(solution)/shard_map/ppermute | solution.py:36
  86.8 1.0 constant_dynamic-update-slice_fusion.3
  87.8 3.2 %collective-permute-start.19 = (bf16[128,6144]{1,0:T(8,128)(2,1)S(1)}, bf16[128,6144]{1,0:T(8,128)(2,1)S(1)}, u32[]{:S(2)}, u32[]{:S(2)}) collective-permute-start(bf16[128,6144]{1,0:T(8,128)(2,1)S(1)} %get-tuple-element.13), channel_id=1, source_target_pairs={{0,48},{1,49},{2,50},{3,51},{4,52},{5,53},{6,54},{7,55},{8,76},{9,... | collective-permute-start | bytes 4718600 | tf_op jit(solution)/shard_map/ppermute | solution.py:36
  91.2 3.3 %collective-permute-start.12 = (bf16[32,6144]{1,0:T(8,128)(2,1)S(1)}, bf16[32,6144]{1,0:T(8,128)(2,1)S(1)}, u32[]{:S(2)}, u32[]{:S(2)}) collective-permute-start(bf16[32,6144]{1,0:T(8,128)(2,1)S(1)} %slice.87), channel_id=1, source_target_pairs={{0,68},{1,69},{2,70},{3,71},{4,0},{5,1},{6,2},{7,3},{8,56},{9,57},... | collective-permute-start | bytes 1179656 | tf_op jit(solution)/shard_map/ppermute | solution.py:36
  94.5 1.1 constant_dynamic-update-slice_fusion.2
  95.6 8.8 %collective-permute-done.11 = bf16[32,6144]{1,0:T(8,128)(2,1)S(1)} collective-permute-done((bf16[32,6144]{1,0:T(8,128)(2,1)S(1)}, bf16[32,6144]{1,0:T(8,128)(2,1)S(1)}, u32[]{:S(2)}, u32[]{:S(2)}) %collective-permute-start.11) | collective-permute-done | bytes 393248 | tf_op jit(solution)/shard_map/ppermute | solution.py:36
  104.3 0.8 constant_dynamic-update-slice_fusion.1
  105.1 0.8 constant_dynamic-update-slice_fusion
  106.0 2.0 collective-permute-start.18
  108.0 4.3 %collective-permute-done.14.refs_1_ = bf16[128,6144]{1,0:T(8,128)(2,1)} collective-permute-done((bf16[128,6144]{1,0:T(8,128)(2,1)S(1)}, bf16[128,6144]{1,0:T(8,128)(2,1)}, u32[]{:S(2)}, u32[]{:S(2)}) %collective-permute-start.14) | collective-permute-done | bytes 1572896 | tf_op jit(solution)/shard_map/ppermute | solution.py:36
  112.5 15.8 %collective-permute-done.15.refs_2_ = bf16[128,6144]{1,0:T(8,128)(2,1)} collective-permute-done((bf16[128,6144]{1,0:T(8,128)(2,1)S(1)}, bf16[128,6144]{1,0:T(8,128)(2,1)}, u32[]{:S(2)}, u32[]{:S(2)}) %collective-permute-start.15) | collective-permute-done | bytes 1572896 | tf_op jit(solution)/shard_map/ppermute | solution.py:36
  128.4 3.8 %collective-permute-start.23 = (bf16[128,6144]{1,0:T(8,128)(2,1)}, bf16[128,6144]{1,0:T(8,128)(2,1)}, u32[]{:S(2)}, u32[]{:S(2)}) collective-permute-start(bf16[128,6144]{1,0:T(8,128)(2,1)} %collective-permute-done.15.refs_2_), channel_id=1, source_target_pairs={{0,48},{1,49},{2,50},{3,51},{4,52},{5,53},{6,54},{7,55},{8,76},{9,... | collective-permute-start | bytes 4718600 | tf_op jit(solution)/shard_map/ppermute | solution.py:36
  133.4 12.6 %collective-permute-done.22.refs_1_ = bf16[128,6144]{1,0:T(8,128)(2,1)} collective-permute-done((bf16[128,6144]{1,0:T(8,128)(2,1)}, bf16[128,6144]{1,0:T(8,128)(2,1)}, u32[]{:S(2)}, u32[]{:S(2)}) %collective-permute-start.22) | collective-permute-done | bytes 1572896 | tf_op jit(solution)/shard_map/ppermute | solution.py:36
  146.6 0.9 squeeze.27.refs_0_
  147.5 0.9 squeeze.28.refs_0_
  148.5 0.9 squeeze.29.refs_0_
  149.5 0.9 squeeze.30.refs_0_
  150.9 12.8 %scored.4 = f32[512,128]{1,0:T(8,128)} custom-call(s32[512,1]{1,0:T(8,128)} %squeeze.27.refs_0_, bf16[256,6144]{1,0:T(8,128)(2,1)} %get-tuple-element.14.refs_1_, bf16[256,6144]{1,0:T(8,128)(2,1)} %collective-permute-done.13.refs_2_, bf16[6144,1024]{1,0:T(8,128)(2,1)} %refs_5_.5), custom_call_target="tpu_custom_call" | custom-call | flops 6442450944 | bytes 18874368 | tf_op jit(solution)/shard_map/scored/pallas_call | solution.py:103
  163.6 12.8 %scored.5 = f32[512,128]{1,0:T(8,128)} custom-call(s32[512,1]{1,0:T(8,128)} %squeeze.28.refs_0_, bf16[128,6144]{1,0:T(8,128)(2,1)} %collective-permute-done.14.refs_1_, bf16[128,6144]{1,0:T(8,128)(2,1)} %collective-permute-done.15.refs_2_, bf16[128,6144]{1,0:T(8,128)(2,1)} %collective-permute-done.16.refs_3_, ...), custom_call_target="tpu_custom_call" | custom-call | flops 6442450944 | bytes 18874368 | tf_op jit(solution)/shard_map/scored/pallas_call | solution.py:103
  176.5 1.1 copy-done.16
  177.6 12.8 %scored.6 = f32[512,128]{1,0:T(8,128)} custom-call(s32[512,1]{1,0:T(8,128)} %squeeze.29.refs_0_, bf16[128,6144]{1,0:T(8,128)(2,1)} %collective-permute-done.18.refs_1_, bf16[128,6144]{1,0:T(8,128)(2,1)} %copy-done.15, bf16[128,6144]{1,0:T(8,128)(2,1)} %collective-permute-done.20.refs_3_, bf16[128,6144]{1,0:T(8,128)(2,1)} %copy-done.16, ...), custom_call_target="tpu_custom_call" | custom-call | flops 6442450944 | bytes 18874368 | tf_op jit(solution)/shard_map/scored/pallas_call | solution.py:103
  190.4 12.9 %scored.7 = f32[512,128]{1,0:T(8,128)} custom-call(s32[512,1]{1,0:T(8,128)} %squeeze.30.refs_0_, bf16[128,6144]{1,0:T(8,128)(2,1)} %collective-permute-done.22.refs_1_, bf16[128,6144]{1,0:T(8,128)(2,1)} %collective-permute-done.23.refs_2_, bf16[128,6144]{1,0:T(8,128)(2,1)} %collective-permute-done.24.refs_3_, ...), custom_call_target="tpu_custom_call" | custom-call | flops 6442450944 | bytes 18874368 | tf_op jit(solution)/shard_map/scored/pallas_call | solution.py:103
  203.3 1.0 pad_maximum_fusion
  204.8 1.0 fusion.22
  205.8 7.3 %all-to-all-start.1 = ((f32[128,1,48]{2,1,0:T(1,128)}), f32[128,1,48]{2,1,0:T(1,128)S(1)}, u32[]{:S(2)}, u32[]{:S(2)}) async-start(f32[128,1,48]{2,1,0:T(1,128)} %bitcast.20), calls=%async_computation.1 | async-start | bytes 131072 | tf_op jit(solution)/shard_map/all_to_all | solution.py:264
  213.7 8.9 %all-to-all-done.1 = f32[128,1,48]{2,1,0:T(1,128)S(1)} async-done(((f32[128,1,48]{2,1,0:T(1,128)}), f32[128,1,48]{2,1,0:T(1,128)S(1)}, u32[]{:S(2)}, u32[]{:S(2)}) %all-to-all-start.1) | async-done | bytes 24608 | tf_op jit(solution)/shard_map/all_to_all | solution.py:264
  (117 shorter events, 11.5 us)
Async XLA Ops:
  0.6 44.0 %copy-start = (bf16[32,768]{1,0:T(8,128)(2,1)S(1)}, bf16[32,768]{1,0:T(8,128)(2,1)}, u32[]{:S(2)}) copy-start(bf16[32,768]{1,0:T(8,128)(2,1)} %param.14) | copy-start | bytes 147460
  2.5 13.2 %collective-permute-start = (bf16[32,1664]{0,1:T(8,128)(2,1)S(1)}, bf16[32,1664]{0,1:T(8,128)(2,1)S(1)}, u32[]{:S(2)}, u32[]{:S(2)}) collective-permute-start(bf16[32,1664]{0,1:T(8,128)(2,1)S(1)} %copy.76), channel_id=1, source_target_pairs={{0,64},{1,65},{2,66},{3,67},{4,68},{5,69},{6,70},{7,71},{8,72},{9,... | collective-permute-start | bytes 319496 | tf_op jit(solution)/shard_map/ppermute | solution.py:36
  15.9 1.8 collective-permute-start.1
  18.2 9.4 %collective-permute-start.2 = (bf16[128,1664]{0,1:T(8,128)(2,1)S(1)}, bf16[128,1664]{0,1:T(8,128)(2,1)S(1)}, u32[]{:S(2)}, u32[]{:S(2)}) collective-permute-start(bf16[128,1664]{0,1:T(8,128)(2,1)S(1)} %pad_maximum_fusion.7), channel_id=1, source_target_pairs={{0,16},{1,17},{2,18},{3,19},{4,20},{5,21},{6,22},{7,23},{8,56},{9,... | collective-permute-start | bytes 1277960 | tf_op jit(solution)/shard_map/ppermute | solution.py:36
  27.6 9.3 %collective-permute-start.4 = (bf16[64,1664]{0,1:T(8,128)(2,1)S(1)}, bf16[64,1664]{0,1:T(8,128)(2,1)S(1)}, u32[]{:S(2)}, u32[]{:S(2)}) collective-permute-start(bf16[64,1664]{0,1:T(8,128)(2,1)S(1)} %bitcast.85), channel_id=1, source_target_pairs={{0,16},{1,17},{2,18},{3,19},{4,20},{5,21},{6,22},{7,23},{8,56},{9,... | collective-permute-start | bytes 638984 | tf_op jit(solution)/shard_map/ppermute | solution.py:36
  27.9 11.6 %collective-permute-start.3 = (bf16[128,1664]{0,1:T(8,128)(2,1)S(1)}, bf16[128,1664]{0,1:T(8,128)(2,1)}, u32[]{:S(2)}, u32[]{:S(2)}) collective-permute-start(bf16[128,1664]{0,1:T(8,128)(2,1)S(1)} %collective-permute-done.2), channel_id=1, source_target_pairs={{0,8},{1,9},{2,10},{3,11},{4,12},{5,13},{6,14},{7,15},{8,0},{9,1},... | collective-permute-start | bytes 1277960 | tf_op jit(solution)/shard_map/ppermute | solution.py:36
  36.9 1.8 copy-start.2
  36.9 1.8 collective-permute-start.5
  38.7 0.8 copy-start.3
  44.5 0.7 copy-start.14
  44.9 8.2 %copy-start.7 = (bf16[16,6144]{1,0:T(8,128)(2,1)S(1)}, bf16[16,6144]{1,0:T(8,128)(2,1)}, u32[]{:S(2)}) copy-start(bf16[16,6144]{1,0:T(8,128)(2,1)} %param.19) | copy-start | bytes 589828
  45.5 7.7 %copy-start.8 = (bf16[16,6144]{1,0:T(8,128)(2,1)S(1)}, bf16[16,6144]{1,0:T(8,128)(2,1)}, u32[]{:S(2)}) copy-start(bf16[16,6144]{1,0:T(8,128)(2,1)} %param.18) | copy-start | bytes 589828
  45.5 7.7 %copy-start.9 = (bf16[16,6144]{1,0:T(8,128)(2,1)S(1)}, bf16[16,6144]{1,0:T(8,128)(2,1)}, u32[]{:S(2)}) copy-start(bf16[16,6144]{1,0:T(8,128)(2,1)} %param.20) | copy-start | bytes 589828
  46.6 12.7 %all-to-all-start = ((bf16[8,4,768]{2,1,0:T(4,128)(2,1)}), bf16[8,4,768]{2,1,0:T(4,128)(2,1)S(1)}, u32[]{:S(2)}, u32[]{:S(2)}) async-start(bf16[8,4,768]{2,1,0:T(4,128)(2,1)} %convert_element_type.47), calls=%async_computation | async-start | bytes 98304 | tf_op jit(solution)/shard_map/all_to_all | solution.py:215
  60.4 0.9 copy-start.1
  60.4 1.2 copy-start.10
  62.4 11.1 %collective-permute-start.6 = (bf16[16,6144]{1,0:T(8,128)(2,1)S(1)}, bf16[16,6144]{1,0:T(8,128)(2,1)S(1)}, u32[]{:S(2)}, u32[]{:S(2)}) collective-permute-start(bf16[16,6144]{1,0:T(8,128)(2,1)S(1)} %get-tuple-element.5), channel_id=1, source_target_pairs={{0,1},{1,2},{2,3},{3,0},{4,5},{5,6},{6,7},{7,4},{8,9},{9,10},{10,1... | collective-permute-start | bytes 589832 | tf_op jit(solution)/shard_map/ppermute | solution.py:36
  62.9 10.5 %collective-permute-start.7 = (bf16[16,6144]{1,0:T(8,128)(2,1)S(1)}, bf16[16,6144]{1,0:T(8,128)(2,1)S(1)}, u32[]{:S(2)}, u32[]{:S(2)}) collective-permute-start(bf16[16,6144]{1,0:T(8,128)(2,1)S(1)} %get-tuple-element.5), channel_id=1, source_target_pairs={{0,3},{1,0},{2,1},{3,2},{4,7},{5,4},{6,5},{7,6},{8,11},{9,8},{10,9... | collective-permute-start | bytes 589832 | tf_op jit(solution)/shard_map/ppermute | solution.py:36
  65.6 7.9 %collective-permute-start.8 = (bf16[16,6144]{1,0:T(8,128)(2,1)S(1)}, bf16[16,6144]{1,0:T(8,128)(2,1)S(1)}, u32[]{:S(2)}, u32[]{:S(2)}) collective-permute-start(bf16[16,6144]{1,0:T(8,128)(2,1)S(1)} %get-tuple-element.5), channel_id=1, source_target_pairs={{0,2},{1,3},{2,0},{3,1},{4,6},{5,7},{6,4},{7,5},{8,10},{9,11},{10,... | collective-permute-start | bytes 589832 | tf_op jit(solution)/shard_map/ppermute | solution.py:36
  73.5 13.3 %collective-permute-start.9 = (bf16[64,6144]{1,0:T(8,128)(2,1)S(1)}, bf16[64,6144]{1,0:T(8,128)(2,1)S(1)}, u32[]{:S(2)}, u32[]{:S(2)}) collective-permute-start(bf16[64,6144]{1,0:T(8,128)(2,1)S(1)} %pad_maximum_fusion.3), channel_id=1, source_target_pairs={{0,4},{1,5},{2,6},{3,7},{4,64},{5,65},{6,66},{7,67},{8,24},{9,25},... | collective-permute-start | bytes 2359304 | tf_op jit(solution)/shard_map/ppermute | solution.py:36
  74.2 16.9 %collective-permute-start.10 = (bf16[64,6144]{1,0:T(8,128)(2,1)S(1)}, bf16[64,6144]{1,0:T(8,128)(2,1)S(1)}, u32[]{:S(2)}, u32[]{:S(2)}) collective-permute-start(bf16[64,6144]{1,0:T(8,128)(2,1)S(1)} %pad_maximum_fusion.3), channel_id=1, source_target_pairs={{0,68},{1,69},{2,70},{3,71},{4,0},{5,1},{6,2},{7,3},{8,56},{9,57},... | collective-permute-start | bytes 2359304 | tf_op jit(solution)/shard_map/ppermute | solution.py:36
  87.8 24.4 %collective-permute-start.14 = (bf16[128,6144]{1,0:T(8,128)(2,1)S(1)}, bf16[128,6144]{1,0:T(8,128)(2,1)}, u32[]{:S(2)}, u32[]{:S(2)}) collective-permute-start(bf16[128,6144]{1,0:T(8,128)(2,1)S(1)} %get-tuple-element.13), channel_id=1, source_target_pairs={{0,16},{1,17},{2,18},{3,19},{4,20},{5,21},{6,22},{7,23},{8,12},{9,... | collective-permute-start | bytes 4718600 | tf_op jit(solution)/shard_map/ppermute | solution.py:36
  87.8 24.4 %collective-permute-start.19 = (bf16[128,6144]{1,0:T(8,128)(2,1)S(1)}, bf16[128,6144]{1,0:T(8,128)(2,1)S(1)}, u32[]{:S(2)}, u32[]{:S(2)}) collective-permute-start(bf16[128,6144]{1,0:T(8,128)(2,1)S(1)} %get-tuple-element.13), channel_id=1, source_target_pairs={{0,48},{1,49},{2,50},{3,51},{4,52},{5,53},{6,54},{7,55},{8,76},{9,... | collective-permute-start | bytes 4718600 | tf_op jit(solution)/shard_map/ppermute | solution.py:36
  91.1 13.3 %collective-permute-start.11 = (bf16[32,6144]{1,0:T(8,128)(2,1)S(1)}, bf16[32,6144]{1,0:T(8,128)(2,1)S(1)}, u32[]{:S(2)}, u32[]{:S(2)}) collective-permute-start(bf16[32,6144]{1,0:T(8,128)(2,1)S(1)} %slice.86), channel_id=1, source_target_pairs={{0,4},{1,5},{2,6},{3,7},{4,64},{5,65},{6,66},{7,67},{8,24},{9,25},... | collective-permute-start | bytes 1179656 | tf_op jit(solution)/shard_map/ppermute | solution.py:36
  91.2 13.9 %collective-permute-start.12 = (bf16[32,6144]{1,0:T(8,128)(2,1)S(1)}, bf16[32,6144]{1,0:T(8,128)(2,1)S(1)}, u32[]{:S(2)}, u32[]{:S(2)}) collective-permute-start(bf16[32,6144]{1,0:T(8,128)(2,1)S(1)} %slice.87), channel_id=1, source_target_pairs={{0,68},{1,69},{2,70},{3,71},{4,0},{5,1},{6,2},{7,3},{8,56},{9,57},... | collective-permute-start | bytes 1179656 | tf_op jit(solution)/shard_map/ppermute | solution.py:36
  95.6 36.6 %copy-start.17 = (s32[4]{0:T(128)S(1)}, s32[4]{0:T(128)}, u32[]{:S(2)}) copy-start(s32[4]{0:T(128)} %constant.108.clone) | copy-start | bytes 52
  95.6 36.8 %copy-start.12 = (s32[4,4]{1,0:T(4,128)S(1)}, s32[4,4]{1,0:T(4,128)}, u32[]{:S(2)}) copy-start(s32[4,4]{1,0:T(4,128)} %constant.109.clone) | copy-start | bytes 196
  95.6 36.8 %copy-start.13 = (s32[4,4]{1,0:T(4,128)S(1)}, s32[4,4]{1,0:T(4,128)}, u32[]{:S(2)}) copy-start(s32[4,4]{1,0:T(4,128)} %constant.110.clone) | copy-start | bytes 196
  95.6 37.1 %copy-start.11 = (s32[2048]{0:T(1024)S(1)}, s32[2048]{0:T(1024)}, u32[]{:S(2)}) copy-start(s32[2048]{0:T(1024)} %param.24) | copy-start | bytes 24580
  106.0 44.4 %collective-permute-start.13 = (bf16[256,6144]{1,0:T(8,128)(2,1)}, bf16[256,6144]{1,0:T(8,128)(2,1)}, u32[]{:S(2)}, u32[]{:S(2)}) collective-permute-start(bf16[256,6144]{1,0:T(8,128)(2,1)} %get-tuple-element.14.refs_1_), channel_id=1, source_target_pairs={{0,8},{1,9},{2,10},{3,11},{4,12},{5,13},{6,14},{7,15},{8,0},{9,1},... | collective-permute-start | bytes 9437192 | tf_op jit(solution)/shard_map/ppermute | solution.py:36
  106.0 22.4 %collective-permute-start.15 = (bf16[128,6144]{1,0:T(8,128)(2,1)S(1)}, bf16[128,6144]{1,0:T(8,128)(2,1)}, u32[]{:S(2)}, u32[]{:S(2)}) collective-permute-start(bf16[128,6144]{1,0:T(8,128)(2,1)S(1)} %get-tuple-element.15), channel_id=1, source_target_pairs={{0,48},{1,49},{2,50},{3,51},{4,52},{5,53},{6,54},{7,55},{8,76},{9,... | collective-permute-start | bytes 4718600 | tf_op jit(solution)/shard_map/ppermute | solution.py:36
  106.0 26.2 %collective-permute-start.18 = (bf16[128,6144]{1,0:T(8,128)(2,1)S(1)}, bf16[128,6144]{1,0:T(8,128)(2,1)}, u32[]{:S(2)}, u32[]{:S(2)}) collective-permute-start(bf16[128,6144]{1,0:T(8,128)(2,1)S(1)} %get-tuple-element.15), channel_id=1, source_target_pairs={{0,16},{1,17},{2,18},{3,19},{4,20},{5,21},{6,22},{7,23},{8,12},{9,... | collective-permute-start | bytes 4718600 | tf_op jit(solution)/shard_map/ppermute | solution.py:36
  112.2 20.6 %collective-permute-start.16 = (bf16[128,6144]{1,0:T(8,128)(2,1)}, bf16[128,6144]{1,0:T(8,128)(2,1)}, u32[]{:S(2)}, u32[]{:S(2)}) collective-permute-start(bf16[128,6144]{1,0:T(8,128)(2,1)} %collective-permute-done.14.refs_1_), channel_id=1, source_target_pairs={{0,8},{1,9},{2,10},{3,11},{4,12},{5,13},{6,14},{7,15},{8,0},{9,1},... | collective-permute-start | bytes 4718600 | tf_op jit(solution)/shard_map/ppermute | solution.py:36
  112.3 51.4 %copy-start.15 = (bf16[128,6144]{1,0:T(8,128)(2,1)}, bf16[128,6144]{1,0:T(8,128)(2,1)S(1)}, u32[]{:S(2)}) copy-start(bf16[128,6144]{1,0:T(8,128)(2,1)S(1)} %collective-permute-done.19.refs_2_) | copy-start | bytes 4718596
  112.3 33.7 %collective-permute-start.22 = (bf16[128,6144]{1,0:T(8,128)(2,1)}, bf16[128,6144]{1,0:T(8,128)(2,1)}, u32[]{:S(2)}, u32[]{:S(2)}) collective-permute-start(bf16[128,6144]{1,0:T(8,128)(2,1)} %collective-permute-done.14.refs_1_), channel_id=1, source_target_pairs={{0,16},{1,17},{2,18},{3,19},{4,20},{5,21},{6,22},{7,23},{8,12},{9,... | collective-permute-start | bytes 4718600 | tf_op jit(solution)/shard_map/ppermute | solution.py:36
  128.4 22.3 %collective-permute-start.23 = (bf16[128,6144]{1,0:T(8,128)(2,1)}, bf16[128,6144]{1,0:T(8,128)(2,1)}, u32[]{:S(2)}, u32[]{:S(2)}) collective-permute-start(bf16[128,6144]{1,0:T(8,128)(2,1)} %collective-permute-done.15.refs_2_), channel_id=1, source_target_pairs={{0,48},{1,49},{2,50},{3,51},{4,52},{5,53},{6,54},{7,55},{8,76},{9,... | collective-permute-start | bytes 4718600 | tf_op jit(solution)/shard_map/ppermute | solution.py:36
  132.2 31.5 %collective-permute-start.17 = (bf16[128,6144]{1,0:T(8,128)(2,1)}, bf16[128,6144]{1,0:T(8,128)(2,1)}, u32[]{:S(2)}, u32[]{:S(2)}) collective-permute-start(bf16[128,6144]{1,0:T(8,128)(2,1)} %collective-permute-done.15.refs_2_), channel_id=1, source_target_pairs={{0,8},{1,9},{2,10},{3,11},{4,12},{5,13},{6,14},{7,15},{8,0},{9,1},... | collective-permute-start | bytes 4718600 | tf_op jit(solution)/shard_map/ppermute | solution.py:36
  132.8 43.7 %collective-permute-start.21 = (bf16[128,6144]{1,0:T(8,128)(2,1)S(1)}, bf16[128,6144]{1,0:T(8,128)(2,1)S(1)}, u32[]{:S(2)}, u32[]{:S(2)}) collective-permute-start(bf16[128,6144]{1,0:T(8,128)(2,1)S(1)} %collective-permute-done.19.refs_2_), channel_id=1, source_target_pairs={{0,8},{1,9},{2,10},{3,11},{4,12},{5,13},{6,14},{7,15},{8,0},{9,1},... | collective-permute-start | bytes 4718600 | tf_op jit(solution)/shard_map/ppermute | solution.py:36
  146.0 30.5 %collective-permute-start.20 = (bf16[128,6144]{1,0:T(8,128)(2,1)}, bf16[128,6144]{1,0:T(8,128)(2,1)}, u32[]{:S(2)}, u32[]{:S(2)}) collective-permute-start(bf16[128,6144]{1,0:T(8,128)(2,1)} %collective-permute-done.18.refs_1_), channel_id=1, source_target_pairs={{0,8},{1,9},{2,10},{3,11},{4,12},{5,13},{6,14},{7,15},{8,0},{9,1},... | collective-permute-start | bytes 4718600 | tf_op jit(solution)/shard_map/ppermute | solution.py:36
  150.3 40.1 %collective-permute-start.24 = (bf16[128,6144]{1,0:T(8,128)(2,1)}, bf16[128,6144]{1,0:T(8,128)(2,1)}, u32[]{:S(2)}, u32[]{:S(2)}) collective-permute-start(bf16[128,6144]{1,0:T(8,128)(2,1)} %collective-permute-done.22.refs_1_), channel_id=1, source_target_pairs={{0,8},{1,9},{2,10},{3,11},{4,12},{5,13},{6,14},{7,15},{8,0},{9,1},... | collective-permute-start | bytes 4718600 | tf_op jit(solution)/shard_map/ppermute | solution.py:36
  150.7 39.8 %collective-permute-start.25 = (bf16[128,6144]{1,0:T(8,128)(2,1)}, bf16[128,6144]{1,0:T(8,128)(2,1)}, u32[]{:S(2)}, u32[]{:S(2)}) collective-permute-start(bf16[128,6144]{1,0:T(8,128)(2,1)} %collective-permute-done.23.refs_2_), channel_id=1, source_target_pairs={{0,8},{1,9},{2,10},{3,11},{4,12},{5,13},{6,14},{7,15},{8,0},{9,1},... | collective-permute-start | bytes 4718600 | tf_op jit(solution)/shard_map/ppermute | solution.py:36
  176.5 1.1 copy-start.16
  190.4 12.9 %copy-start.4 = (f32[512,128]{1,0:T(8,128)S(1)}, f32[512,128]{1,0:T(8,128)}, u32[]{:S(2)}) copy-start(f32[512,128]{1,0:T(8,128)} %scored.4) | copy-start | bytes 786436
  190.4 12.9 %copy-start.5 = (f32[512,128]{1,0:T(8,128)S(1)}, f32[512,128]{1,0:T(8,128)}, u32[]{:S(2)}) copy-start(f32[512,128]{1,0:T(8,128)} %scored.5) | copy-start | bytes 786436
  190.4 12.9 %copy-start.6 = (f32[512,128]{1,0:T(8,128)S(1)}, f32[512,128]{1,0:T(8,128)}, u32[]{:S(2)}) copy-start(f32[512,128]{1,0:T(8,128)} %scored.6) | copy-start | bytes 786436
  205.8 16.8 %all-to-all-start.1 = ((f32[128,1,48]{2,1,0:T(1,128)}), f32[128,1,48]{2,1,0:T(1,128)S(1)}, u32[]{:S(2)}, u32[]{:S(2)}) async-start(f32[128,1,48]{2,1,0:T(1,128)} %bitcast.20), calls=%async_computation.1 | async-start | bytes 131072 | tf_op jit(solution)/shard_map/all_to_all | solution.py:264
